TPU v7x, 32 devices: a whole 2x2x4 slice. The times are simulated.
32 devices in a mesh: expert: 8 (over z, x), hidden: 4 (over y, core).
Axes of the slice: x: 2, y: 2, z: 4, core: 2. Of those that a mesh axis runs over, the one named last changes fastest.
Arguments:
- tokens: bfloat16 [16384, 768], P(('expert', 'hidden')), may hold values from -6 to 6
- doc_lengths: int32 [8, 3], P('expert'), may hold values from 1 to 1024, 2048 in all within a row
- expert_ids: int32 [16384, 2], P(('expert', 'hidden')), may hold values from 0 to 7, all different within a row; in each aligned block of 512 rows (0 to 511, 512 to 1023, ...) at most 160 rows name the same one
- gain_one: float32 [768], replicated, may hold values from 0.5 to 1.5
- shift_one: float32 [768], replicated, may hold values from -1.25 to 1.25
- w_query: bfloat16 [768, 768], replicated, may hold values from -0.21875 to 0.21875
- w_key: bfloat16 [768, 768], replicated, may hold values from -0.21875 to 0.21875
- w_value: bfloat16 [768, 768], replicated, may hold values from -0.21875 to 0.21875
- w_out: bfloat16 [768, 768], replicated, may hold values from -3.5 to 3.5
- gain_two: float32 [768], replicated, may hold values from 0.5 to 1.5
- shift_two: float32 [768], replicated, may hold values from -1.25 to 1.25
- w_router: bfloat16 [768, 8], replicated, may hold values from -0.21875 to 0.21875
- w_up: bfloat16 [8, 768, 3072], P('expert', None, 'hidden'), may hold values from -0.21875 to 0.21875
- w_down: bfloat16 [8, 3072, 768], P('expert', 'hidden'), may hold values from -0.109375 to 0.109375
- out_grad: bfloat16 [16384, 768], P(('expert', 'hidden')), may hold values from -6 to 6
Outputs:
- output: bfloat16 [16384, 768], P(('expert', 'hidden'))
- input_grad: bfloat16 [16384, 768], P(('expert', 'hidden'))
- gain_one_grad: float32 [768], replicated
- shift_one_grad: float32 [768], replicated
- w_query_grad: float32 [768, 768], replicated
- w_key_grad: float32 [768, 768], replicated
- w_value_grad: float32 [768, 768], replicated
- w_out_grad: float32 [768, 768], replicated
- gain_two_grad: float32 [768], replicated
- shift_two_grad: float32 [768], replicated
- w_router_grad: float32 [768, 8], replicated
- w_up_grad: float32 [8, 768, 3072], P('expert', None, 'hidden')
- w_down_grad: float32 [8, 3072, 768], P('expert', 'hidden')
- load: float32 [8], replicated
Inputs may be any that keep to these rules, and one draw needn't show every extreme that they name: `doc_lengths`: the lengths of a group's documents, in order; they sum to 2048 and the longest in every group is 1024. `expert_ids`: each token names 2 different experts; among the 512 tokens of one device no expert is named more than 160 times, and in every draw some expert is named exactly 160 times by one device.
All inputs are finite; a program needn't handle non-finite values.
Results may differ from a plain program's by a relative error of at most 0.019.
Values may be sent and summed in bfloat16 or wider, within the bound.
A program may use at most 192 MiB of HBM per device.

v0:
```python
from functools import partial
import jax
import jax.numpy as jnp
from jax import lax
from jax.sharding import PartitionSpec as P

HEADS = 12
HEAD_DIM = 64
EPSILON = 1e-05
SCALE = 0.125
MASKED = -1e30
EXACT = lax.Precision.HIGHEST


def product(left, right):
    return jnp.dot(left, right, preferred_element_type=jnp.float32)


def contract(left, right, left_axis, right_axis):
    return lax.dot_general(
        left, right, (((left_axis,), (right_axis,)), ((), ())), preferred_element_type=jnp.float32
    )


def norm_parts(values):
    row_mean = jnp.mean(values, axis=-1, keepdims=True)
    centred = values - row_mean
    inverse = lax.rsqrt(jnp.mean(centred * centred, axis=-1, keepdims=True) + EPSILON)
    return (centred * inverse, inverse)


def norm_back(grad_out, normed, inverse, gain):
    grad_normed = grad_out * gain
    first_mean = jnp.mean(grad_normed, axis=-1, keepdims=True)
    second_mean = jnp.mean(grad_normed * normed, axis=-1, keepdims=True)
    return inverse * (grad_normed - first_mean - normed * second_mean)


def gelu_back(pre_act, grad_hidden):
    unused, pull = jax.vjp(partial(jax.nn.gelu, approximate=True), pre_act)
    return pull(grad_hidden)[0]


def split_heads(array):
    return array.reshape(array.shape[0], HEADS, HEAD_DIM).transpose(1, 0, 2)


def join_heads(array):
    return array.transpose(1, 0, 2).reshape(array.shape[1], HEADS * HEAD_DIM)


def shards(
    tokens,
    doc_lengths,
    expert_ids,
    gain_one,
    shift_one,
    w_query,
    w_key,
    w_value,
    w_out,
    gain_two,
    shift_two,
    w_router,
    w_up,
    w_down,
    out_grad,
):
    row_count = tokens.shape[0]
    model_width = tokens.shape[1]
    top_count = expert_ids.shape[1]
    experts = lax.axis_size("expert") * w_up.shape[0]
    capacity = max(2, row_count * top_count * 5 // (4 * experts))
    input_float = tokens.astype(jnp.float32)
    normed_one, inverse_one = norm_parts(input_float)
    h_one = (normed_one * gain_one + shift_one).astype(jnp.bfloat16)
    queries = product(h_one, w_query).astype(jnp.bfloat16)
    key_proj = product(h_one, w_key).astype(jnp.bfloat16)
    value_proj = product(h_one, w_value).astype(jnp.bfloat16)
    all_keys, all_values = (
        lax.all_gather(key_proj, "hidden", axis=0, tiled=True),
        lax.all_gather(value_proj, "hidden", axis=0, tiled=True),
    )
    key_count = all_keys.shape[0]
    doc_ends = jnp.cumsum(doc_lengths[0])
    query_pos = lax.axis_index("hidden") * row_count + jnp.arange(row_count, dtype=jnp.int32)
    key_pos = jnp.arange(key_count, dtype=jnp.int32)
    query_doc = jnp.sum((query_pos[:, None] >= doc_ends[None, :]).astype(jnp.int32), axis=1)
    key_doc = jnp.sum((key_pos[:, None] >= doc_ends[None, :]).astype(jnp.int32), axis=1)
    allowed = (query_doc[:, None] == key_doc[None, :]) & (key_pos[None, :] <= query_pos[:, None])

    def head_forward(pieces):
        q_head, k_head, v_head = pieces
        scores = jnp.where(allowed, contract(q_head, k_head, 1, 1) * SCALE, MASKED)
        top_score = jnp.max(scores, axis=1, keepdims=True)
        expd = jnp.exp(scores - top_score)
        row_total = jnp.sum(expd, axis=1, keepdims=True)
        weights = (expd / row_total).astype(jnp.bfloat16)
        return (product(weights, v_head), (top_score + jnp.log(row_total))[:, 0])

    mixture, log_total = lax.map(
        head_forward, (split_heads(queries), split_heads(all_keys), split_heads(all_values))
    )
    attended = join_heads(mixture).astype(jnp.bfloat16)
    residual = input_float + product(attended, w_out)
    normed_two, inverse_two = norm_parts(residual)
    h_two = (normed_two * gain_two + shift_two).astype(jnp.bfloat16)
    h_two_float = h_two.astype(jnp.float32)
    router_float = w_router.astype(jnp.float32)
    logits = jnp.dot(h_two_float, router_float, precision=EXACT)
    choose_table = (
        expert_ids[:, :, None] == jnp.arange(experts, dtype=jnp.int32)[None, None, :]
    ).astype(jnp.float32)
    chosen = jnp.sum(choose_table * logits[:, None, :], axis=2)
    gate_weights = jax.nn.softmax(chosen, axis=1)
    flat_ids = expert_ids.reshape(-1)
    onehot = choose_table.reshape(-1, experts).astype(jnp.int32)
    before = jnp.cumsum(onehot, axis=0) - onehot
    slot_index = jnp.sum(before * onehot, axis=1)
    counts = jnp.sum(choose_table, axis=(0, 1))
    outgoing = (
        jnp.zeros((experts, capacity, model_width), jnp.bfloat16)
        .at[flat_ids, slot_index]
        .set(jnp.repeat(h_two, top_count, axis=0))
    )
    slot_rows = lax.all_to_all(outgoing, "expert", split_axis=0, concat_axis=0, tiled=True).reshape(
        -1, model_width
    )
    rows_all = lax.all_gather(slot_rows, "hidden", axis=0, tiled=True)
    pre_act = product(rows_all, w_up[0])
    hidden_act = jax.nn.gelu(pre_act, approximate=True).astype(jnp.bfloat16)
    partial_sum = product(hidden_act, w_down[0])
    produced = lax.psum_scatter(
        partial_sum.astype(jnp.bfloat16), "hidden", scatter_dimension=0, tiled=True
    )
    returned = lax.all_to_all(
        produced.reshape(-1, capacity, model_width),
        "expert",
        split_axis=0,
        concat_axis=0,
        tiled=True,
    )
    returned_rows = (
        returned[flat_ids, slot_index]
        .reshape(row_count, top_count, model_width)
        .astype(jnp.float32)
    )
    expert_mix = jnp.sum(gate_weights[:, :, None] * returned_rows, axis=1)
    output = (residual + expert_mix).astype(jnp.bfloat16)
    grad_output = out_grad.astype(jnp.float32)
    grad_returned = (gate_weights[:, :, None] * grad_output[:, None, :]).astype(jnp.bfloat16)
    grad_gates = jnp.sum(returned_rows * grad_output[:, None, :], axis=2)
    grad_chosen = gate_weights * (
        grad_gates - jnp.sum(gate_weights * grad_gates, axis=1, keepdims=True)
    )
    grad_logits = jnp.sum(grad_chosen[:, :, None] * choose_table, axis=1)
    router_grad = jnp.dot(h_two_float.T, grad_logits, precision=EXACT)
    grad_h_two = jnp.dot(grad_logits, router_float.T, precision=EXACT)
    grad_outgoing = (
        jnp.zeros((experts, capacity, model_width), jnp.bfloat16)
        .at[flat_ids, slot_index]
        .set(grad_returned.reshape(-1, model_width))
    )
    grad_slots = lax.all_to_all(
        grad_outgoing, "expert", split_axis=0, concat_axis=0, tiled=True
    ).reshape(-1, model_width)
    trainable = (lax.axis_index("expert") >= experts // 2).astype(jnp.float32)
    grad_all = lax.all_gather(grad_slots, "hidden", axis=0, tiled=True)
    grad_hidden = contract(grad_all, w_down[0], 1, 1)
    down_grad = contract(hidden_act, grad_all, 0, 0)
    grad_pre = gelu_back(pre_act, grad_hidden).astype(jnp.bfloat16)
    up_grad = contract(rows_all, grad_pre, 0, 0)
    partial_in = contract(grad_pre, w_up[0], 1, 1)
    grad_in = lax.psum_scatter(
        partial_in.astype(jnp.bfloat16), "hidden", scatter_dimension=0, tiled=True
    )
    up_grad = up_grad[None] * trainable
    down_grad = down_grad[None] * trainable
    grad_back = lax.all_to_all(
        grad_in.reshape(-1, capacity, model_width),
        "expert",
        split_axis=0,
        concat_axis=0,
        tiled=True,
    )
    grad_h_two = grad_h_two + jnp.sum(
        grad_back[flat_ids, slot_index]
        .reshape(row_count, top_count, model_width)
        .astype(jnp.float32),
        axis=1,
    )
    gain_two_grad = jnp.sum(grad_h_two * normed_two, axis=0)
    shift_two_grad = jnp.sum(grad_h_two, axis=0)
    grad_residual = grad_output + norm_back(grad_h_two, normed_two, inverse_two, gain_two)
    grad_branch = grad_residual.astype(jnp.bfloat16)
    out_proj_grad = contract(attended, grad_branch, 0, 0)
    grad_attended = contract(grad_branch, w_out, 1, 1).astype(jnp.bfloat16)
    back_keys, back_values = (all_keys, all_values)

    def head_backward(pieces):
        q_head, k_head, v_head, g_head, head_total = pieces
        scores = jnp.where(allowed, contract(q_head, k_head, 1, 1) * SCALE, MASKED)
        weights = jnp.exp(scores - head_total[:, None])
        grad_weights = contract(g_head, v_head, 1, 1)
        grad_scores = (
            weights * (grad_weights - jnp.sum(weights * grad_weights, axis=1, keepdims=True))
        ).astype(jnp.bfloat16)
        grad_query = product(grad_scores, k_head) * SCALE
        grad_key = contract(grad_scores, q_head, 0, 0) * SCALE
        grad_value = contract(weights.astype(jnp.bfloat16), g_head, 0, 0)
        return (grad_query, grad_key, grad_value)

    grad_query, grad_key, grad_value = lax.map(
        head_backward,
        (
            split_heads(queries),
            split_heads(back_keys),
            split_heads(back_values),
            split_heads(grad_attended),
            log_total,
        ),
    )
    grad_key, grad_value = (
        lax.psum_scatter(
            join_heads(grad_key).astype(jnp.bfloat16), "hidden", scatter_dimension=0, tiled=True
        ).astype(jnp.float32),
        lax.psum_scatter(
            join_heads(grad_value).astype(jnp.bfloat16), "hidden", scatter_dimension=0, tiled=True
        ).astype(jnp.float32),
    )
    grad_query = join_heads(grad_query).astype(jnp.bfloat16)
    grad_key = grad_key.astype(jnp.bfloat16)
    grad_value = grad_value.astype(jnp.bfloat16)
    query_grad = contract(h_one, grad_query, 0, 0)
    key_grad = contract(h_one, grad_key, 0, 0)
    value_grad = contract(h_one, grad_value, 0, 0)
    grad_h_one = (
        contract(grad_query, w_query, 1, 1)
        + contract(grad_key, w_key, 1, 1)
        + contract(grad_value, w_value, 1, 1)
    )
    gain_one_grad = jnp.sum(grad_h_one * normed_one, axis=0)
    shift_one_grad = jnp.sum(grad_h_one, axis=0)
    input_grad = (grad_residual + norm_back(grad_h_one, normed_one, inverse_one, gain_one)).astype(
        jnp.bfloat16
    )
    totals = lax.psum(
        (
            gain_one_grad,
            shift_one_grad,
            query_grad,
            key_grad,
            value_grad,
            out_proj_grad,
            gain_two_grad,
            shift_two_grad,
            router_grad,
            counts,
        ),
        ("expert", "hidden"),
    )
    total_tokens = row_count * lax.axis_size("expert") * lax.axis_size("hidden")
    load = totals[9] * experts / (total_tokens * top_count)
    return (
        output,
        input_grad,
        totals[0],
        totals[1],
        totals[2],
        totals[3],
        totals[4],
        totals[5],
        totals[6],
        totals[7],
        totals[8],
        up_grad,
        down_grad,
        load,
    )


def solution(mesh):
    in_specs = (
        P(("expert", "hidden"), None),
        P("expert", None),
        P(("expert", "hidden"), None),
        P(),
        P(),
        P(),
        P(),
        P(),
        P(),
        P(),
        P(),
        P(),
        P("expert", None, "hidden"),
        P("expert", "hidden", None),
        P(("expert", "hidden"), None),
    )
    out_specs = (
        P(("expert", "hidden"), None),
        P(("expert", "hidden"), None),
        P(),
        P(),
        P(),
        P(),
        P(),
        P(),
        P(),
        P(),
        P(),
        P("expert", None, "hidden"),
        P("expert", "hidden", None),
        P(),
    )
    return jax.shard_map(shards, mesh=mesh, in_specs=in_specs, out_specs=out_specs, check_vma=False)
```

profile of v0, /device:TPU:0, one launch (start us, length us, event | category | flops | bytes accessed | tf_op | source)
XLA Modules:
  0.0 1053.0 jit_solution(8360045255467511472)
XLA Ops:
  10.2 3.5 convolution_convert_fusion.4
  32.1 13.0 %all-gather.5.cloned.1.call-done = bf16[2048,768]{1,0:T(8,128)(2,1)} async-done(((bf16[512,768]{1,0:T(8,128)(2,1)}), bf16[2048,768]{1,0:T(8,128)(2,1)}) %all-gather.5.cloned.1.call-update) | async-done | bytes 3145744 | tf_op jit(solution)/shard_map/all_gather | solution.py:81
  45.1 4.8 copy.68
  49.9 6.7 copy.71
  56.6 19.4 %all-gather.7.cloned.1.call-done = bf16[2048,768]{1,0:T(8,128)(2,1)} async-done(((bf16[512,768]{1,0:T(8,128)(2,1)}), bf16[2048,768]{1,0:T(8,128)(2,1)}) %all-gather.7.cloned.1.call-update) | async-done | bytes 3145744 | tf_op jit(solution)/shard_map/all_gather | solution.py:82
  76.0 4.7 copy.69
  80.7 6.5 copy.72
  88.2 85.5 %while.28 = (s32[]{:T(128)}, bf16[12,512,64]{1,2,0:T(8,128)(2,1)}, f32[12,512]{1,0:T(8,128)}, bf16[12,512,64]{2,1,0:T(8,128)(2,1)S(1)}, bf16[12,2048,64]{2,1,0:T...) while((s32[]{:T(128)}, bf16[12,512,64]{1,2,0:T(8,128)(2,1)}, ...), condition=%wide.region_8.9_spmd.clone, body=%wide.region_5.8_spmd.clone.sunk | while | flops 279969280 | bytes 13928569 | solution.py:101
  98.3 2.7 fusion.149
  105.4 2.7 fusion.149
  112.6 2.7 fusion.149
  119.7 2.7 fusion.149
  126.8 2.7 fusion.149
  133.9 2.7 fusion.149
  141.1 2.7 fusion.149
  155.3 2.7 fusion.149
  169.5 2.7 fusion.149
  173.6 3.0 fusion.95
  181.0 7.7 scatter_custom_fusion
  188.8 51.8 %all_to_all.20 = bf16[8,160,768]{2,1,0:T(8,128)(2,1)} all-to-all(bf16[8,160,768]{2,1,0:T(8,128)(2,1)} %bitcast.191), channel_id=1, replica_groups=mesh['expert'=8,'hidden'=4] {'expert'}, dimensions={0} | all-to-all | bytes 3932160 | tf_op jit(solution)/shard_map/all_to_all | solution.py:126
  244.2 5.5 mul.265
  250.5 7.0 scatter_custom_fusion.1
  257.5 48.8 %all_to_all.21 = bf16[8,160,768]{2,1,0:T(8,128)(2,1)} all-to-all(bf16[8,160,768]{2,1,0:T(8,128)(2,1)S(1)} %bitcast.190), channel_id=1, replica_groups=mesh['expert'=8,'hidden'=4] {'expert'}, dimensions={0} | all-to-all | bytes 3932160 | tf_op jit(solution)/shard_map/all_to_all | solution.py:164
  306.6 12.8 %fusion.72 = f32[5120,768]{1,0:T(8,128)} fusion(bf16[5120,768]{1,0:T(8,128)(2,1)} %all-gather.9.cloned.1.call-done, bf16[1,768,768]{2,1,0:T(8,128)(2,1)S(1)} %copy-done), kind=kOutput, calls=%fused_computation.115 | convolution fusion | flops 6039797760 | bytes 24772608 | tf_op jit(solution)/shard_map/dot_general | solution.py:16
  319.4 40.1 %all-gather.11.cloned.1.call-done = bf16[5120,768]{1,0:T(8,128)(2,1)} async-done(((bf16[1280,768]{1,0:T(8,128)(2,1)}), bf16[5120,768]{1,0:T(8,128)(2,1)}) %all-gather.11.cloned.1.call-update) | async-done | bytes 7864336 | tf_op jit(solution)/shard_map/all_gather | solution.py:168
  359.5 19.0 %fusion.50 = bf16[5120,768]{1,0:T(8,128)(2,1)S(1)} fusion(f32[5120,768]{1,0:T(8,128)} %fusion.72, bf16[5120,768]{1,0:T(8,128)(2,1)} %all-gather.11.cloned.1.call-done, bf16[1,768,768]{2,1,0:T(8,128)(2,1)S(1)} %copy-done.40), kind=kOutput, calls=%fused_computation.67 | convolution fusion | flops 6118440960 | bytes 32636928 | tf_op jit(solution)/shard_map/dot_general | solution.py:20
  378.5 3.1 copy-done.48
  381.7 8.7 convolution_convert_fusion
  390.5 14.8 %convolution_convert_fusion.1 = bf16[5120,768]{1,0:T(8,128)(2,1)} fusion(bf16[1,768,768]{2,1,0:T(8,128)(2,1)S(1)} %copy-done.40, f32[5120,768]{1,0:T(8,128)} %fusion.72), kind=kOutput, calls=%fused_computation.70 | convolution fusion | flops 6079119360 | bytes 24772608 | tf_op jit(solution)/shard_map/dot_general | solution.py:16
  405.3 54.2 %reduce-scatter.7.cloned.1.call-done = bf16[1280,768]{1,0:T(8,128)(2,1)} async-done(((bf16[5120,768]{1,0:T(8,128)(2,1)}), bf16[1280,768]{1,0:T(8,128)(2,1)}) %reduce-scatter.7.cloned.1.call-update) | async-done | bytes 1966096 | tf_op jit(solution)/shard_map/reduce_scatter | solution.py:174
  459.5 5.5 all-to-all-start.3
  465.0 66.1 %reduce-scatter.5.cloned.1.call-done = bf16[1280,768]{1,0:T(8,128)(2,1)} async-done(((bf16[5120,768]{1,0:T(8,128)(2,1)}), bf16[1280,768]{1,0:T(8,128)(2,1)}) %reduce-scatter.5.cloned.1.call-update) | async-done | bytes 1966096 | tf_op jit(solution)/shard_map/reduce_scatter | solution.py:133
  531.1 5.6 all-to-all-start.1
  538.1 14.3 %gather_fusion.1 = bf16[1024,768]{1,0:T(8,128)(2,1)} fusion(bf16[8,160,768]{2,1,0:T(8,128)(2,1)S(1)} %all-to-all-done.3, s32[1024]{0:T(1024)S(1)} %bitcast.184), kind=kCustom, calls=%fused_computation.1 | custom fusion | bytes 3153920 | tf_op jit(solution)/shard_map/gather | solution.py:187
  552.4 4.9 reshape.365
  557.3 25.0 %all-to-all-done.1 = bf16[8,160,768]{2,1,0:T(8,128)(2,1)} async-done(((bf16[8,160,768]{2,1,0:T(8,128)(2,1)}), bf16[8,160,768]{2,1,0:T(8,128)(2,1)}, u32[]{:S(2)}, u32[]{:S(2)}) %all-to-all-start.1) | async-done | bytes 1966112 | tf_op jit(solution)/shard_map/all_to_all | solution.py:136
  582.3 19.8 %gather_fusion = bf16[1024,768]{1,0:T(8,128)(2,1)} fusion(bf16[8,160,768]{2,1,0:T(8,128)(2,1)} %all-to-all-done.1, s32[1024]{0:T(1024)S(1)} %bitcast.185), kind=kCustom, calls=%fused_computation | custom fusion | bytes 3153920 | tf_op jit(solution)/shard_map/gather | solution.py:144
  602.1 3.5 reshape.364
  605.6 9.5 multiply_reduce_fusion.1
  616.4 5.7 reduce_sum.241
  626.7 132.8 %while.29 = (s32[]{:T(128)}, bf16[12,512,64]{1,2,0:T(8,128)(2,1)S(1)}, bf16[12,2048,64]{1,2,0:T(8,128)(2,1)}, bf16[12,2048,64]{1,2,0:T(8,128)(2,1)}, bf16[12,512...) while((s32[]{:T(128)}, ...), condition=%wide.region_30.31_spmd.clone, body=%wide.region_28.30_spmd.clone.sunk | while | flops 683834880 | bytes 34630792 | solution.py:213
  629.3 2.9 multiply_reduce_fusion.11
  640.3 2.9 multiply_reduce_fusion.11
  651.4 3.0 multiply_reduce_fusion.11
  662.4 3.0 multiply_reduce_fusion.11
  673.5 3.0 multiply_reduce_fusion.11
  684.6 3.0 multiply_reduce_fusion.11
  695.7 2.9 multiply_reduce_fusion.11
  706.7 3.0 multiply_reduce_fusion.11
  717.8 2.9 multiply_reduce_fusion.11
  728.9 2.9 multiply_reduce_fusion.11
  739.9 2.9 multiply_reduce_fusion.11
  751.0 3.0 multiply_reduce_fusion.11
  761.0 3.7 fusion.89
  766.8 28.9 %reduce-scatter.9.cloned.1.call-done = bf16[512,768]{0,1:T(8,128)(2,1)} async-done(((bf16[2048,768]{0,1:T(8,128)(2,1)}), bf16[512,768]{0,1:T(8,128)(2,1)}) %reduce-scatter.9.cloned.1.call-update) | async-done | bytes 786448 | tf_op jit(solution)/shard_map/reduce_scatter | solution.py:224
  795.7 3.6 fusion.87
  799.3 37.1 %reduce-scatter.11.cloned.1.call-done = bf16[512,768]{0,1:T(8,128)(2,1)} async-done(((bf16[2048,768]{0,1:T(8,128)(2,1)}), bf16[512,768]{0,1:T(8,128)(2,1)}) %reduce-scatter.11.cloned.1.call-update) | async-done | bytes 786448 | tf_op jit(solution)/shard_map/reduce_scatter | solution.py:227
  836.4 3.6 fusion.85
  840.0 12.2 %multiply_bitcast_fusion.1 = f32[1,768,768]{2,1,0:T(8,128)} fusion(bf16[5120,768]{1,0:T(8,128)(2,1)} %all-gather.9.cloned.1.call-done, bf16[5120,768]{1,0:T(8,128)(2,1)} %copy-done.48, f32[]{:T(128)S(6)} %convert_element_type.180), kind=kOutput, calls=%fused_computation.78 | convolution fusion | flops 6040387584 | bytes 18087940 | tf_op jit(solution)/shard_map/dot_general | solution.py:20
  852.2 14.4 %multiply_bitcast_fusion = f32[1,768,768]{2,1,0:T(8,128)} fusion(bf16[5120,768]{1,0:T(8,128)(2,1)} %all-gather.11.cloned.1.call-done, f32[]{:T(128)S(6)} %convert_element_type.180, f32[5120,768]{1,0:T(8,128)} %fusion.72), kind=kOutput, calls=%fused_computation.77 | convolution fusion | flops 6075777024 | bytes 25952260 | tf_op jit(solution)/shard_map/dot_general | solution.py:20
  872.6 41.3 %all-reduce = (f32[768]{0:T(1024)}, f32[768]{0:T(1024)}, f32[768]{0:T(1024)}, f32[768]{0:T(1024)}, f32[768,8]{0,1:T(8,128)}, /*index=5*/f32[8]{0:T(128)S(1)}) all-reduce(f32[768]{0:T(1024)S(1)} %get-tuple-element.230, f32[768]{0:T(1024)S(1)} %get-tuple-element.235, ...), channel_id=1, replica_groups=mesh['expert'=8,'hidden'=4] {'expert','hidden'}, use_global_device_ids=true, to_apply=%region_36.37 | all-reduce | flops 9224 | bytes 73792 | tf_op jit(solution)/shard_map/psum | solution.py:247
  914.4 2.9 fusion.63
  917.3 119.2 %all-reduce.4.cloned.1.call-done = (f32[768,768]{1,0:T(8,128)}, f32[768,768]{1,0:T(8,128)}, f32[768,768]{1,0:T(8,128)}, f32[768,768]{1,0:T(8,128)}) async-done(((f32[768,768]{1,0:T(8,128)}, f32[768,768]{1,0:T(8,128)}, f32[768,768]{1,0:T(8,128)}, f32[768,768]{1,0:T(8,128)}), (f32[768,768]{1,0:T(8,128)}, f32[768,768]{1,0:T(8,128)}, f32[768,768]{1,0:T(8,128)}, ...) | async-done | bytes 9437200 | tf_op jit(solution)/shard_map/psum | solution.py:247
  1036.5 3.4 copy.121
  (306 shorter events, 212.7 us)
Async XLA Ops:
  7.2 299.4 %copy-start = (bf16[1,768,768]{2,1,0:T(8,128)(2,1)S(1)}, bf16[1,768,768]{2,1,0:T(8,128)(2,1)}, u32[]{:S(2)}) copy-start(bf16[1,768,768]{2,1,0:T(8,128)(2,1)} %param.31) | copy-start | bytes 3538948
  7.2 37.9 %all-gather.5.cloned.1.call-start = ((), (), s32[]{:S(2)}) async-start(), calls=%async_computation.8 | async-start | bytes 3932160 | tf_op jit(solution)/shard_map/all_gather | solution.py:81
  8.6 12.4 %copy-start.26 = (f32[512]{0:T(512)}, f32[512]{0:T(512)S(1)}, u32[]{:S(2)}) copy-start(f32[512]{0:T(512)S(1)} %broadcast_multiply_fusion.5) | copy-start | bytes 6148
  10.2 10.9 %copy-start.30 = (f32[512]{0:T(512)}, f32[512]{0:T(512)S(1)}, u32[]{:S(2)}) copy-start(f32[512]{0:T(512)S(1)} %add_rsqrt_fusion.1) | copy-start | bytes 6148
  10.2 3.6 copy-start.4
  10.2 3.6 copy-start.17
  10.2 3.6 copy-start.32
  10.2 3.6 copy-start.45
  13.7 2.3 copy-start.25
  13.7 3.6 copy-start.47
  13.7 62.2 %all-gather.7.cloned.1.call-start = ((), (), s32[]{:S(2)}) async-start(), calls=%async_computation.9 | async-start | bytes 3932160 | tf_op jit(solution)/shard_map/all_gather | solution.py:82
  15.7 290.9 %all-gather.9.cloned.1.call-start = ((), (), s32[]{:S(2)}) async-start(), calls=%async_computation.10 | async-start | bytes 9830400 | tf_op jit(solution)/shard_map/all_gather | solution.py:129
  20.3 0.6 copy-start.22
  23.2 3.2 copy-start.39
  26.4 5.1 copy-start.34
  80.7 7.5 copy-start.35
  173.6 3.0 copy-start.12
  173.6 4.7 copy-start.24
  173.6 4.7 copy-start.38
  176.7 1.1 copy-start.2
  177.8 0.6 copy-start.28
  178.7 71.0 %copy-start.6 = (bf16[512,768]{1,0:T(8,128)(2,1)}, bf16[512,768]{1,0:T(8,128)(2,1)S(1)}, u32[]{:S(2)}) copy-start(bf16[512,768]{1,0:T(8,128)(2,1)S(1)} %add_convert_fusion.1) | copy-start | bytes 2359300
  240.6 1.1 copy-start.8
  240.6 118.9 %all-gather.11.cloned.1.call-start = ((), (), s32[]{:S(2)}) async-start(), calls=%async_computation.12 | async-start | bytes 9830400 | tf_op jit(solution)/shard_map/all_gather | solution.py:168
  244.2 5.5 copy-start.23
  306.3 53.2 %copy-start.40 = (bf16[1,768,768]{2,1,0:T(8,128)(2,1)S(1)}, bf16[1,768,768]{2,1,0:T(8,128)(2,1)}, u32[]{:S(2)}) copy-start(bf16[1,768,768]{2,1,0:T(8,128)(2,1)} %param.32) | copy-start | bytes 3538948
  306.3 153.2 %reduce-scatter.7.cloned.1.call-start = ((), (), s32[]{:S(2)}) async-start(), calls=%async_computation.13 | async-start | bytes 9830400 | tf_op jit(solution)/shard_map/reduce_scatter | solution.py:174
  378.5 3.2 copy-start.48
  390.4 140.7 %reduce-scatter.5.cloned.1.call-start = ((), (), s32[]{:S(2)}) async-start(), calls=%async_computation.11 | async-start | bytes 9830400 | tf_op jit(solution)/shard_map/reduce_scatter | solution.py:133
  459.5 71.6 %all-to-all-start.3 = ((bf16[8,160,768]{2,1,0:T(8,128)(2,1)}), bf16[8,160,768]{2,1,0:T(8,128)(2,1)S(1)}, u32[]{:S(2)}, u32[]{:S(2)}) async-start(bf16[8,160,768]{2,1,0:T(8,128)(2,1)} %bitcast.199), calls=%async_computation.5 | async-start | bytes 3932160 | tf_op jit(solution)/shard_map/all_to_all | solution.py:179
  531.1 5.7 copy-start.9
  531.1 51.2 %all-to-all-start.1 = ((bf16[8,160,768]{2,1,0:T(8,128)(2,1)}), bf16[8,160,768]{2,1,0:T(8,128)(2,1)}, u32[]{:S(2)}, u32[]{:S(2)}) async-start(bf16[8,160,768]{2,1,0:T(8,128)(2,1)} %bitcast.198), calls=%async_computation.2 | async-start | bytes 3932160 | tf_op jit(solution)/shard_map/all_to_all | solution.py:136
  536.8 258.9 %reduce-scatter.9.cloned.1.call-start = ((), (), s32[]{:S(2)}) async-start(), calls=%async_computation.14 | async-start | bytes 3932160 | tf_op jit(solution)/shard_map/reduce_scatter | solution.py:224
  616.3 5.7 copy-start.3
  616.3 5.8 copy-start.29
  622.1 1.4 copy-start.10
  622.1 1.6 copy-start.11
  623.8 1.4 copy-start.41
  626.0 0.7 copy-start.36
  626.0 0.7 copy-start.37
  759.5 0.9 copy-start.20
  759.5 1.4 copy-start.5
  759.5 1.4 copy-start.27
  759.5 1.4 copy-start.31
  759.6 1.4 copy-start.33
  759.6 1.4 copy-start.46
  759.6 76.8 %reduce-scatter.11.cloned.1.call-start = ((), (), s32[]{:S(2)}) async-start(), calls=%async_computation.15 | async-start | bytes 3932160 | tf_op jit(solution)/shard_map/reduce_scatter | solution.py:227
  760.4 276.1 %all-reduce.4.cloned.1.call-start = ((), (), s32[]{:S(2)}) async-start(), calls=%async_computation.16 | async-start | bytes 18874368 | tf_op jit(solution)/shard_map/psum | solution.py:247
  760.9 3.7 copy-start.13
  852.2 14.4 %copy-start.7 = (bf16[512,768]{1,0:T(8,128)(2,1)S(1)}, bf16[512,768]{1,0:T(8,128)(2,1)}, u32[]{:S(2)}) copy-start(bf16[512,768]{1,0:T(8,128)(2,1)} %copy-done.6) | copy-start | bytes 2359300
  852.2 14.8 %copy-start.21 = (bf16[12,512,64]{1,2,0:T(8,128)(2,1)S(1)}, bf16[12,512,64]{1,2,0:T(8,128)(2,1)}, u32[]{:S(2)}) copy-start(bf16[12,512,64]{1,2,0:T(8,128)(2,1)} %copy-done.20) | copy-start | bytes 2359300
  852.2 14.8 %copy-start.42 = (bf16[768,768]{1,0:T(8,128)(2,1)S(1)}, bf16[768,768]{1,0:T(8,128)(2,1)}, u32[]{:S(2)}) copy-start(bf16[768,768]{1,0:T(8,128)(2,1)} %param.24) | copy-start | bytes 3538948
  867.0 1.3 copy-start.43
  867.0 1.5 copy-start.44
  868.5 1.3 copy-start.18
  868.5 1.5 copy-start.19
  1036.5 3.4 copy-start.16
  1039.8 2.5 copy-start.15
  1042.4 2.5 copy-start.14
  1042.4 3.9 copy-start.1
Sparse Core Ops, SparseCore 0:
  13.8 31.2 all-gather.4
  47.2 28.6 all-gather.6
  240.7 53.0 all-gather.8
  306.4 53.0 all-gather.10
  390.5 68.9 reduce-scatter.6
  462.1 68.9 reduce-scatter.4
  759.6 36.0 reduce-scatter.8
  798.4 37.9 reduce-scatter.10
  843.2 193.2 all-reduce.3
where the time goes:
time: 1060 us; the launch traced here: 1050 us
  waiting for transfers between devices  404 us (38%)
  matrix products  292 us (28%)
  blocking collectives  142 us (13%)
  local copies, waits for them, and re-layouts  134 us (13%)
  other arithmetic  54.7 us (5%)
  between operations  14.7 us (1%)
  starting transfers between devices  11.9 us (1%)
    dot_general x72, matrix products, contract(): lax.dot_general(left, right, (((left_axis,), (right_axis,)), ((), ())), p...  197 us
    psum x1, waiting for transfers between devices, shards(): lax.psum((gain_one_grad, shift_one_grad, query_grad, key_grad, value_grad...  119 us
    dot_general x30, matrix products, product(): return jnp.dot(left, right, preferred_element_type=jnp.float32)  92.8 us
    reduce_scatter x1, waiting for transfers between devices, shards(): lax.psum_scatter(partial_sum.astype(jnp.bfloat16), 'hidden', scatter_dime...  66.1 us
    reduce_scatter x1, waiting for transfers between devices, shards(): lax.psum_scatter(partial_in.astype(jnp.bfloat16), 'hidden', scatter_dimen...  54.2 us
    all_to_all x1, blocking collectives, shards(): lax.all_to_all(outgoing, 'expert', split_axis=0, concat_axis=0, tiled=True)  51.8 us
    all_to_all x1, blocking collectives, shards(): lax.all_to_all(grad_outgoing, 'expert', split_axis=0, concat_axis=0, tile...  48.8 us
    unnamed x107, local copies, waits for them, and re-layouts  41.6 us
  transfers between devices with their start and end apart: 11, of which 9 were waited for; matrix products, arithmetic and copies ran while one was open for 13% of the time, Pallas kernels for 0%

commit v1 on v0

--- a/solution.py
+++ b/solution.py
@@ -10,6 +10,11 @@
 SCALE = 0.125
 MASKED = -1e30
 EXACT = lax.Precision.HIGHEST
+
+
+def swapped_in(block, axis, along):
+    sent = jnp.stack([block] * lax.axis_size(axis))
+    return jnp.concatenate(lax.all_to_all(sent, axis, 0, 0), axis=along)
 
 
 def product(left, right):
@@ -79,7 +84,7 @@
     value_proj = product(h_one, w_value).astype(jnp.bfloat16)
     all_keys, all_values = (
         lax.all_gather(key_proj, "hidden", axis=0, tiled=True),
-        lax.all_gather(value_proj, "hidden", axis=0, tiled=True),
+        swapped_in(value_proj, "hidden", 0),
     )
     key_count = all_keys.shape[0]
     doc_ends = jnp.cumsum(doc_lengths[0])

time: 1060 us -> 1080 us (1.019)
    all_to_all x0 -> x1, waiting for transfers between devices: none -> 37.2 us  [swapped_in(): return jnp.concatenate(lax.all_to_all(sent, axis, 0, 0), axis=along)]
    all_gather x1 -> x0, waiting for transfers between devices: 19.4 us -> none  [shards(): lax.all_gather(value_proj, 'hidden', axis=0, tiled=True)]
    all_gather x1, waiting for transfers between devices: 13 us -> 0.01 us  [shards(): lax.all_gather(key_proj, 'hidden', axis=0, tiled=True)]
  transfers between devices with their start and end apart: 11 -> 11, of which waited for: 9 -> 8; matrix products, arithmetic and copies ran while one was open for 13% -> 14% of each run, Pallas kernels for 0% -> 0%
where the time goes in v1:
time: 1080 us; the launch traced here: 1070 us
  waiting for transfers between devices  409 us (38%)
  matrix products  292 us (27%)
  local copies, waits for them, and re-layouts  144 us (13%)
  blocking collectives  142 us (13%)
  other arithmetic  54.7 us (5%)
  starting transfers between devices  16.6 us (2%)
  between operations  15 us (1%)
    dot_general x72, matrix products, contract(): lax.dot_general(left, right, (((left_axis,), (right_axis,)), ((), ())), p...  197 us
    psum x1, waiting for transfers between devices, shards(): lax.psum((gain_one_grad, shift_one_grad, query_grad, key_grad, value_grad...  119 us
    dot_general x30, matrix products, product(): return jnp.dot(left, right, preferred_element_type=jnp.float32)  93 us
    reduce_scatter x1, waiting for transfers between devices, shards(): lax.psum_scatter(partial_sum.astype(jnp.bfloat16), 'hidden', scatter_dime...  66.1 us
    reduce_scatter x1, waiting for transfers between devices, shards(): lax.psum_scatter(partial_in.astype(jnp.bfloat16), 'hidden', scatter_dimen...  54.2 us
    all_to_all x1, blocking collectives, shards(): lax.all_to_all(outgoing, 'expert', split_axis=0, concat_axis=0, tiled=True)  51.5 us
    all_to_all x1, blocking collectives, shards(): lax.all_to_all(grad_outgoing, 'expert', split_axis=0, concat_axis=0, tile...  48.8 us
    psum x1, blocking collectives, shards(): lax.psum((gain_one_grad, shift_one_grad, query_grad, key_grad, value_grad...  41.3 us
  transfers between devices with their start and end apart: 11, of which 8 were waited for; matrix products, arithmetic and copies ran while one was open for 14% of the time, Pallas kernels for 0%

profile of v1, /device:TPU:0, one launch (start us, length us, event | category | flops | bytes accessed | tf_op | source)
XLA Modules:
  0.0 1072.9 jit_solution(9123067136643722671)
XLA Ops:
  10.2 3.5 convolution_convert_fusion.4
  18.9 4.8 all-to-all-start
  40.2 37.2 %all-to-all-done = bf16[4,512,768]{1,2,0:T(8,128)(2,1)} async-done(((bf16[4,512,768]{1,2,0:T(8,128)(2,1)}), bf16[4,512,768]{1,2,0:T(8,128)(2,1)}, u32[]{:S(2)}, u32[]{:S(2)}) %all-to-all-start) | async-done | bytes 3145760 | tf_op jit(solution)/shard_map/all_to_all | solution.py:17
  77.3 6.0 copy.87
  83.4 6.1 reshape_reshape.4
  89.5 6.6 copy.90
  96.0 4.7 copy.85
  100.8 6.5 copy.89
  108.2 85.5 %while.28 = (s32[]{:T(128)}, bf16[12,512,64]{1,2,0:T(8,128)(2,1)}, f32[12,512]{1,0:T(8,128)}, bf16[12,512,64]{2,1,0:T(8,128)(2,1)S(1)}, bf16[12,2048,64]{2,1,0:T...) while((s32[]{:T(128)}, bf16[12,512,64]{1,2,0:T(8,128)(2,1)}, ...), condition=%wide.region_8.9_spmd.clone, body=%wide.region_5.8_spmd.clone.sunk | while | flops 279969280 | bytes 13928569 | solution.py:106
  111.3 2.7 fusion.149
  118.4 2.7 fusion.149
  125.5 2.7 fusion.149
  139.8 2.7 fusion.149
  154.0 2.7 fusion.149
  168.3 2.7 fusion.149
  182.5 2.7 fusion.149
  189.6 2.7 fusion.149
  193.7 3.0 fusion.95
  201.1 7.4 scatter_custom_fusion
  208.5 51.5 %all_to_all.25 = bf16[8,160,768]{2,1,0:T(8,128)(2,1)} all-to-all(bf16[8,160,768]{2,1,0:T(8,128)(2,1)} %bitcast.191), channel_id=1, replica_groups=mesh['expert'=8,'hidden'=4] {'expert'}, dimensions={0} | all-to-all | bytes 3932160 | tf_op jit(solution)/shard_map/all_to_all | solution.py:131
  263.7 5.5 mul.265
  269.9 7.0 scatter_custom_fusion.1
  277.0 48.8 %all_to_all.26 = bf16[8,160,768]{2,1,0:T(8,128)(2,1)} all-to-all(bf16[8,160,768]{2,1,0:T(8,128)(2,1)S(1)} %bitcast.190), channel_id=1, replica_groups=mesh['expert'=8,'hidden'=4] {'expert'}, dimensions={0} | all-to-all | bytes 3932160 | tf_op jit(solution)/shard_map/all_to_all | solution.py:169
  325.9 13.0 %fusion.72 = f32[5120,768]{1,0:T(8,128)} fusion(bf16[5120,768]{1,0:T(8,128)(2,1)} %all-gather.6.cloned.1.call-done, bf16[1,768,768]{2,1,0:T(8,128)(2,1)S(1)} %copy-done), kind=kOutput, calls=%fused_computation.115 | convolution fusion | flops 6039797760 | bytes 24772608 | tf_op jit(solution)/shard_map/dot_general | solution.py:21
  338.9 40.1 %all-gather.8.cloned.1.call-done = bf16[5120,768]{1,0:T(8,128)(2,1)} async-done(((bf16[1280,768]{1,0:T(8,128)(2,1)}), bf16[5120,768]{1,0:T(8,128)(2,1)}) %all-gather.8.cloned.1.call-update) | async-done | bytes 7864336 | tf_op jit(solution)/shard_map/all_gather | solution.py:173
  379.0 19.0 %fusion.50 = bf16[5120,768]{1,0:T(8,128)(2,1)S(1)} fusion(f32[5120,768]{1,0:T(8,128)} %fusion.72, bf16[5120,768]{1,0:T(8,128)(2,1)} %all-gather.8.cloned.1.call-done, bf16[1,768,768]{2,1,0:T(8,128)(2,1)S(1)} %copy-done.40), kind=kOutput, calls=%fused_computation.67 | convolution fusion | flops 6118440960 | bytes 32636928 | tf_op jit(solution)/shard_map/dot_general | solution.py:25
  398.0 3.1 copy-done.48
  401.1 8.8 convolution_convert_fusion
  410.0 14.8 %convolution_convert_fusion.1 = bf16[5120,768]{1,0:T(8,128)(2,1)} fusion(bf16[1,768,768]{2,1,0:T(8,128)(2,1)S(1)} %copy-done.40, f32[5120,768]{1,0:T(8,128)} %fusion.72), kind=kOutput, calls=%fused_computation.70 | convolution fusion | flops 6079119360 | bytes 24772608 | tf_op jit(solution)/shard_map/dot_general | solution.py:21
  424.8 54.2 %reduce-scatter.7.cloned.1.call-done = bf16[1280,768]{1,0:T(8,128)(2,1)} async-done(((bf16[5120,768]{1,0:T(8,128)(2,1)}), bf16[1280,768]{1,0:T(8,128)(2,1)}) %reduce-scatter.7.cloned.1.call-update) | async-done | bytes 1966096 | tf_op jit(solution)/shard_map/reduce_scatter | solution.py:179
  479.1 5.5 all-to-all-start.4
  484.6 66.1 %reduce-scatter.5.cloned.1.call-done = bf16[1280,768]{1,0:T(8,128)(2,1)} async-done(((bf16[5120,768]{1,0:T(8,128)(2,1)}), bf16[1280,768]{1,0:T(8,128)(2,1)}) %reduce-scatter.5.cloned.1.call-update) | async-done | bytes 1966096 | tf_op jit(solution)/shard_map/reduce_scatter | solution.py:138
  550.6 5.6 all-to-all-start.2
  557.6 14.4 %gather_fusion.1 = bf16[1024,768]{1,0:T(8,128)(2,1)} fusion(bf16[8,160,768]{2,1,0:T(8,128)(2,1)S(1)} %all-to-all-done.4, s32[1024]{0:T(1024)S(1)} %bitcast.184), kind=kCustom, calls=%fused_computation.1 | custom fusion | bytes 3153920 | tf_op jit(solution)/shard_map/gather | solution.py:192
  572.0 4.9 reshape.362
  576.8 25.0 %all-to-all-done.2 = bf16[8,160,768]{2,1,0:T(8,128)(2,1)} async-done(((bf16[8,160,768]{2,1,0:T(8,128)(2,1)}), bf16[8,160,768]{2,1,0:T(8,128)(2,1)}, u32[]{:S(2)}, u32[]{:S(2)}) %all-to-all-start.2) | async-done | bytes 1966112 | tf_op jit(solution)/shard_map/all_to_all | solution.py:141
  601.8 19.8 %gather_fusion = bf16[1024,768]{1,0:T(8,128)(2,1)} fusion(bf16[8,160,768]{2,1,0:T(8,128)(2,1)} %all-to-all-done.2, s32[1024]{0:T(1024)S(1)} %bitcast.185), kind=kCustom, calls=%fused_computation | custom fusion | bytes 3153920 | tf_op jit(solution)/shard_map/gather | solution.py:149
  621.6 3.5 reshape.361
  625.1 9.5 multiply_reduce_fusion.1
  635.9 5.7 reduce_sum.241
  646.3 132.8 %while.29 = (s32[]{:T(128)}, bf16[12,512,64]{1,2,0:T(8,128)(2,1)S(1)}, bf16[12,2048,64]{1,2,0:T(8,128)(2,1)}, bf16[12,2048,64]{1,2,0:T(8,128)(2,1)}, bf16[12,512...) while((s32[]{:T(128)}, ...), condition=%wide.region_30.31_spmd.clone, body=%wide.region_28.30_spmd.clone.sunk | while | flops 683834880 | bytes 34630792 | solution.py:218
  648.8 3.0 multiply_reduce_fusion.11
  659.9 3.0 multiply_reduce_fusion.11
  670.9 2.9 multiply_reduce_fusion.11
  682.0 3.0 multiply_reduce_fusion.11
  693.1 3.0 multiply_reduce_fusion.11
  704.1 3.0 multiply_reduce_fusion.11
  715.2 2.9 multiply_reduce_fusion.11
  726.3 3.0 multiply_reduce_fusion.11
  737.4 2.9 multiply_reduce_fusion.11
  748.4 2.9 multiply_reduce_fusion.11
  759.5 2.9 multiply_reduce_fusion.11
  770.5 3.0 multiply_reduce_fusion.11
  780.5 3.7 fusion.89
  786.4 28.9 %reduce-scatter.9.cloned.1.call-done = bf16[512,768]{0,1:T(8,128)(2,1)} async-done(((bf16[2048,768]{0,1:T(8,128)(2,1)}), bf16[512,768]{0,1:T(8,128)(2,1)}) %reduce-scatter.9.cloned.1.call-update) | async-done | bytes 786448 | tf_op jit(solution)/shard_map/reduce_scatter | solution.py:229
  815.3 3.6 fusion.87
  818.9 37.1 %reduce-scatter.11.cloned.1.call-done = bf16[512,768]{0,1:T(8,128)(2,1)} async-done(((bf16[2048,768]{0,1:T(8,128)(2,1)}), bf16[512,768]{0,1:T(8,128)(2,1)}) %reduce-scatter.11.cloned.1.call-update) | async-done | bytes 786448 | tf_op jit(solution)/shard_map/reduce_scatter | solution.py:232
  855.9 3.6 fusion.85
  859.6 12.2 %multiply_bitcast_fusion.1 = f32[1,768,768]{2,1,0:T(8,128)} fusion(bf16[5120,768]{1,0:T(8,128)(2,1)} %all-gather.6.cloned.1.call-done, bf16[5120,768]{1,0:T(8,128)(2,1)} %copy-done.48, f32[]{:T(128)S(6)} %convert_element_type.180), kind=kOutput, calls=%fused_computation.78 | convolution fusion | flops 6040387584 | bytes 18087940 | tf_op jit(solution)/shard_map/dot_general | solution.py:25
  871.8 14.4 %multiply_bitcast_fusion = f32[1,768,768]{2,1,0:T(8,128)} fusion(bf16[5120,768]{1,0:T(8,128)(2,1)} %all-gather.8.cloned.1.call-done, f32[]{:T(128)S(6)} %convert_element_type.180, f32[5120,768]{1,0:T(8,128)} %fusion.72), kind=kOutput, calls=%fused_computation.77 | convolution fusion | flops 6075777024 | bytes 25952260 | tf_op jit(solution)/shard_map/dot_general | solution.py:25
  892.2 41.3 %all-reduce = (f32[768]{0:T(1024)}, f32[768]{0:T(1024)}, f32[768]{0:T(1024)}, f32[768]{0:T(1024)}, f32[768,8]{0,1:T(8,128)}, /*index=5*/f32[8]{0:T(128)S(1)}) all-reduce(f32[768]{0:T(1024)S(1)} %get-tuple-element.251, f32[768]{0:T(1024)S(1)} %get-tuple-element.256, ...), channel_id=1, replica_groups=mesh['expert'=8,'hidden'=4] {'expert','hidden'}, use_global_device_ids=true, to_apply=%region_36.37 | all-reduce | flops 9224 | bytes 73792 | tf_op jit(solution)/shard_map/psum | solution.py:252
  934.0 2.9 fusion.63
  936.8 119.2 %all-reduce.4.cloned.1.call-done = (f32[768,768]{1,0:T(8,128)}, f32[768,768]{1,0:T(8,128)}, f32[768,768]{1,0:T(8,128)}, f32[768,768]{1,0:T(8,128)}) async-done(((f32[768,768]{1,0:T(8,128)}, f32[768,768]{1,0:T(8,128)}, f32[768,768]{1,0:T(8,128)}, f32[768,768]{1,0:T(8,128)}), (f32[768,768]{1,0:T(8,128)}, f32[768,768]{1,0:T(8,128)}, f32[768,768]{1,0:T(8,128)}, ...) | async-done | bytes 9437200 | tf_op jit(solution)/shard_map/psum | solution.py:252
  1056.0 3.4 copy.139
  (308 shorter events, 218.7 us)
Async XLA Ops:
  7.2 318.7 %copy-start = (bf16[1,768,768]{2,1,0:T(8,128)(2,1)S(1)}, bf16[1,768,768]{2,1,0:T(8,128)(2,1)}, u32[]{:S(2)}) copy-start(bf16[1,768,768]{2,1,0:T(8,128)(2,1)} %param.31) | copy-start | bytes 3538948
  7.2 88.8 %all-gather.4.cloned.1.call-start = ((), (), s32[]{:S(2)}) async-start(), calls=%async_computation.9 | async-start | bytes 3932160 | tf_op jit(solution)/shard_map/all_gather | solution.py:86
  8.6 20.6 %copy-start.26 = (f32[512]{0:T(512)}, f32[512]{0:T(512)S(1)}, u32[]{:S(2)}) copy-start(f32[512]{0:T(512)S(1)} %broadcast_multiply_fusion.5) | copy-start | bytes 6148
  10.2 19.1 %copy-start.30 = (f32[512]{0:T(512)}, f32[512]{0:T(512)S(1)}, u32[]{:S(2)}) copy-start(f32[512]{0:T(512)S(1)} %add_rsqrt_fusion.1) | copy-start | bytes 6148
  10.2 3.5 copy-start.4
  10.2 3.5 copy-start.17
  10.2 3.5 copy-start.32
  10.2 3.5 copy-start.45
  18.9 5.3 copy-start.25
  18.9 6.6 copy-start.47
  18.9 58.4 %all-to-all-start = ((bf16[4,512,768]{1,2,0:T(8,128)(2,1)}), bf16[4,512,768]{1,2,0:T(8,128)(2,1)}, u32[]{:S(2)}, u32[]{:S(2)}) async-start(bf16[4,512,768]{1,2,0:T(8,128)(2,1)} %stack.2), calls=%async_computation | async-start | bytes 6291456 | tf_op jit(solution)/shard_map/all_to_all | solution.py:17
  23.7 302.2 %all-gather.6.cloned.1.call-start = ((), (), s32[]{:S(2)}) async-start(), calls=%async_computation.10 | async-start | bytes 9830400 | tf_op jit(solution)/shard_map/all_gather | solution.py:134
  28.5 0.6 copy-start.22
  31.4 3.0 copy-start.39
  34.5 5.1 copy-start.34
  100.8 7.5 copy-start.35
  193.7 3.0 copy-start.12
  193.7 4.7 copy-start.24
  193.7 4.7 copy-start.38
  196.8 1.1 copy-start.2
  197.9 0.6 copy-start.28
  198.8 70.4 %copy-start.6 = (bf16[512,768]{1,0:T(8,128)(2,1)}, bf16[512,768]{1,0:T(8,128)(2,1)S(1)}, u32[]{:S(2)}) copy-start(bf16[512,768]{1,0:T(8,128)(2,1)S(1)} %add_convert_fusion.1) | copy-start | bytes 2359300
  260.0 1.1 copy-start.8
  260.1 118.9 %all-gather.8.cloned.1.call-start = ((), (), s32[]{:S(2)}) async-start(), calls=%async_computation.12 | async-start | bytes 9830400 | tf_op jit(solution)/shard_map/all_gather | solution.py:173
  263.7 5.5 copy-start.23
  325.8 53.2 %copy-start.40 = (bf16[1,768,768]{2,1,0:T(8,128)(2,1)S(1)}, bf16[1,768,768]{2,1,0:T(8,128)(2,1)}, u32[]{:S(2)}) copy-start(bf16[1,768,768]{2,1,0:T(8,128)(2,1)} %param.32) | copy-start | bytes 3538948
  325.8 153.3 %reduce-scatter.7.cloned.1.call-start = ((), (), s32[]{:S(2)}) async-start(), calls=%async_computation.13 | async-start | bytes 9830400 | tf_op jit(solution)/shard_map/reduce_scatter | solution.py:179
  398.0 3.2 copy-start.48
  409.9 140.7 %reduce-scatter.5.cloned.1.call-start = ((), (), s32[]{:S(2)}) async-start(), calls=%async_computation.11 | async-start | bytes 9830400 | tf_op jit(solution)/shard_map/reduce_scatter | solution.py:138
  479.1 71.6 %all-to-all-start.4 = ((bf16[8,160,768]{2,1,0:T(8,128)(2,1)}), bf16[8,160,768]{2,1,0:T(8,128)(2,1)S(1)}, u32[]{:S(2)}, u32[]{:S(2)}) async-start(bf16[8,160,768]{2,1,0:T(8,128)(2,1)} %bitcast.199), calls=%async_computation.6 | async-start | bytes 3932160 | tf_op jit(solution)/shard_map/all_to_all | solution.py:184
  550.6 5.7 copy-start.9
  550.6 51.2 %all-to-all-start.2 = ((bf16[8,160,768]{2,1,0:T(8,128)(2,1)}), bf16[8,160,768]{2,1,0:T(8,128)(2,1)}, u32[]{:S(2)}, u32[]{:S(2)}) async-start(bf16[8,160,768]{2,1,0:T(8,128)(2,1)} %bitcast.198), calls=%async_computation.3 | async-start | bytes 3932160 | tf_op jit(solution)/shard_map/all_to_all | solution.py:141
  556.3 259.0 %reduce-scatter.9.cloned.1.call-start = ((), (), s32[]{:S(2)}) async-start(), calls=%async_computation.14 | async-start | bytes 3932160 | tf_op jit(solution)/shard_map/reduce_scatter | solution.py:229
  635.9 5.7 copy-start.3
  635.9 5.8 copy-start.29
  641.6 1.4 copy-start.10
  641.7 1.6 copy-start.11
  643.3 1.4 copy-start.41
  645.6 0.7 copy-start.36
  645.6 0.7 copy-start.37
  779.0 0.9 copy-start.20
  779.1 1.4 copy-start.5
  779.1 1.4 copy-start.27
  779.1 1.4 copy-start.31
  779.1 1.4 copy-start.33
  779.1 1.4 copy-start.46
  779.1 76.8 %reduce-scatter.11.cloned.1.call-start = ((), (), s32[]{:S(2)}) async-start(), calls=%async_computation.15 | async-start | bytes 3932160 | tf_op jit(solution)/shard_map/reduce_scatter | solution.py:232
  780.0 276.1 %all-reduce.4.cloned.1.call-start = ((), (), s32[]{:S(2)}) async-start(), calls=%async_computation.16 | async-start | bytes 18874368 | tf_op jit(solution)/shard_map/psum | solution.py:252
  780.5 3.7 copy-start.13
  871.8 14.4 %copy-start.7 = (bf16[512,768]{1,0:T(8,128)(2,1)S(1)}, bf16[512,768]{1,0:T(8,128)(2,1)}, u32[]{:S(2)}) copy-start(bf16[512,768]{1,0:T(8,128)(2,1)} %copy-done.6) | copy-start | bytes 2359300
  871.8 14.8 %copy-start.21 = (bf16[12,512,64]{1,2,0:T(8,128)(2,1)S(1)}, bf16[12,512,64]{1,2,0:T(8,128)(2,1)}, u32[]{:S(2)}) copy-start(bf16[12,512,64]{1,2,0:T(8,128)(2,1)} %copy-done.20) | copy-start | bytes 2359300
  871.8 14.8 %copy-start.42 = (bf16[768,768]{1,0:T(8,128)(2,1)S(1)}, bf16[768,768]{1,0:T(8,128)(2,1)}, u32[]{:S(2)}) copy-start(bf16[768,768]{1,0:T(8,128)(2,1)} %param.24) | copy-start | bytes 3538948
  886.6 1.3 copy-start.43
  886.6 1.5 copy-start.44
  888.1 1.3 copy-start.18
  888.1 1.5 copy-start.19
  1056.0 3.4 copy-start.16
  1059.4 2.5 copy-start.15
  1061.9 2.5 copy-start.14
  1061.9 3.9 copy-start.1
Sparse Core Ops, SparseCore 0:
  13.8 47.3 all-gather.3
  260.2 53.1 all-gather.5
  325.9 53.0 all-gather.7
  410.0 68.9 reduce-scatter.6
  481.6 68.9 reduce-scatter.4
  779.2 36.0 reduce-scatter.8
  818.0 37.9 reduce-scatter.10
  862.7 193.2 all-reduce.3
